TPU v7x, 32 devices: a whole 2x2x4 slice. The times are simulated.
32 devices in a mesh: dom: 8 (over y, x, core), sub: 4 (over z).
Axes of the slice: x: 2, y: 2, z: 4, core: 2. Of those that a mesh axis runs over, the one named last changes fastest.
Arguments:
- adjoint_rhs: float32 [384, 320], P(('dom', 'sub')), may hold values from -6 to 6
- adjoint_start: float32 [384, 320], P(('dom', 'sub')), may hold values from -6 to 6
- offdiag_blocks: bfloat16 [6, 384, 320, 320], P(None, ('dom', 'sub')), may hold values from -0.125 to 0.125
- diag_inverse: float32 [384, 320, 320], P(('dom', 'sub')), may hold values from -0.3125 to 0.3125
- geometry_jac: bfloat16 [384, 24, 320], P(('dom', 'sub')), may hold values from -0.125 to 0.125
- neighbor: int32 [384, 6], P(('dom', 'sub')), may hold values from -1 to 383, as said below
- corner_node: int32 [384, 8], P(('dom', 'sub')), may hold values from 0 to 566, as said below
- deform_place: int32 [567], replicated, may hold values from 0 to 575, as said below
- stiff_diag: float32 [3, 3, 576], P(None, None, ('dom', 'sub')), may hold values from -3.5 to 3.5
- stiff_upper: float32 [3, 3, 576], P(None, None, ('dom', 'sub')), may hold values from -3.5 to 3.5
- stiff_lower: float32 [3, 3, 576], P(None, None, ('dom', 'sub')), may hold values from -3.5 to 3.5
Outputs:
- adjoint: float32 [384, 320], P(('dom', 'sub'))
- shape_grad: float32 [3, 576], P(None, ('dom', 'sub'))
Inputs may be any that keep to these rules, and one draw needn't show every extreme that they name: Elements are numbered device by device in the order of dom then sub, 12 to a device. The relation is symmetric: neighbor[e, k] = f >= 0 implies neighbor[f, k xor 1] = e. A neighbour across face 0 or 1 lies on the same device or on the device one step up (face 0) or down (face 1) along dom with the same sub index; across face 2 or 3 on the same device or one step up (face 2) or down (face 3) along sub; across faces 4 and 5 on the same device. At most 12 faces 0 of one device, and as many faces 1, lead to another device, and at most 6 faces 2, and as many faces 3; these counts are reached. `corner_node`: elements that share a corner name the same node. `deform_place`: the positions are distinct.
All inputs are finite; a program needn't handle non-finite values.
Results may differ from a plain program's by a relative error of at most 0.0042.
Values sent between devices are 32-bit elements; how exact they have to be, the bound alone decides.
No kernel may reach another device: no remote copies, remote signals or barrier semaphores. Data moves between devices by JAX's collectives and lax.ppermute only.
A program may use at most 128 MiB of HBM per device.

v0:
```python
import jax
import jax.numpy as jnp
from jax import lax
from jax.sharding import PartitionSpec as P

NF = 6
BX = 1
BY = 2
BZ = 6
SWEEPS = 2
precise = lax.Precision.HIGHEST


def passed_along(value, axis, steps):
    count = lax.axis_size(axis)
    initial, last = (max(0, -steps), min(count, count - steps))
    return lax.ppermute(value, axis, [(source, source + steps) for source in range(initial, last)])


def padded_2(block, sides, width):
    for axis, dim in sides:
        count = lax.axis_size(axis)
        forward = [(i, i + 1) for i in range(count - 1)]
        backward = [(target, source) for source, target in forward]
        low = lax.ppermute(
            lax.slice_in_dim(block, block.shape[dim] - width, None, axis=dim), axis, forward
        )
        high = lax.ppermute(lax.slice_in_dim(block, 0, width, axis=dim), axis, backward)
        block = jnp.concatenate([low, block, high], axis=dim)
    return block


def dom_move(packed, offset):
    return passed_along(packed, "dom", offset)


def sub_move(packed, offset):
    return passed_along(packed, "sub", offset)


def slot_tables(neighbor, remote, capacity, face_index):
    face_ids = neighbor[:, face_index]
    chosen = remote[:, face_index]
    earlier = chosen[None, :] & (face_ids[None, :] < face_ids[:, None])
    send_rank = jnp.sum(earlier.astype(jnp.int32), 1)
    slot_range = jnp.arange(capacity, dtype=jnp.int32)
    send_table = (chosen[:, None] & (send_rank[:, None] == slot_range[None, :])).astype(jnp.float32)
    receive_rank = jnp.cumsum(chosen.astype(jnp.int32)) - 1
    receive_table = (chosen[:, None] & (receive_rank[:, None] == slot_range[None, :])).astype(
        jnp.float32
    )
    return (send_table, receive_table)


def on_device(
    adjoint_rhs,
    adjoint_start,
    offdiag_blocks,
    diag_inverse,
    geometry_jac,
    neighbor,
    corner_node,
    deform_place,
    stiff_diag,
    stiff_upper,
    stiff_lower,
):
    elem_count = adjoint_rhs.shape[0]
    block_size = adjoint_rhs.shape[1]
    device = lax.axis_index(("dom", "sub"))
    first_id = device * elem_count
    has_face = neighbor >= 0
    inside = has_face & (neighbor >= first_id) & (neighbor < first_id + elem_count)
    remote = has_face & jnp.logical_not(inside)
    target = jnp.where(inside, neighbor - first_id, elem_count)
    columns = jnp.arange(elem_count, dtype=jnp.int32)
    local_map = (
        (target.T[:, :, None] == columns[None, None, :])
        .astype(jnp.float32)
        .reshape(NF * elem_count, elem_count)
    )
    tables = [
        slot_tables(neighbor, remote, BY * BZ, 0),
        slot_tables(neighbor, remote, BY * BZ, 1),
        slot_tables(neighbor, remote, BX * BZ, 2),
        slot_tables(neighbor, remote, BX * BZ, 3),
    ]
    adjoint = adjoint_start
    for sweep_index in range(SWEEPS):
        rounded = adjoint.astype(jnp.bfloat16)
        face_terms = jnp.einsum(
            "keij,ei->kej", offdiag_blocks, rounded, preferred_element_type=jnp.float32
        )
        stacked_terms = face_terms.reshape(NF * elem_count, block_size)
        carried = jnp.dot(local_map.T, stacked_terms, precision=precise)
        for face_index in range(4):
            packed = jnp.dot(tables[face_index][0].T, face_terms[face_index], precision=precise)
            if face_index < 2:
                arrived = dom_move(packed, 1 - 2 * face_index)
            else:
                arrived = sub_move(packed, 5 - 2 * face_index)
            carried = carried + jnp.dot(tables[face_index ^ 1][1], arrived, precision=precise)
        adjoint = jnp.einsum("eij,ej->ei", diag_inverse, adjoint_rhs - carried, precision=precise)
    rounded = adjoint.astype(jnp.bfloat16)
    corner_terms = jnp.einsum(
        "emi,ei->em", geometry_jac, rounded, preferred_element_type=jnp.float32
    )
    values = corner_terms.reshape(elem_count, 8, 3).transpose(2, 0, 1).reshape(3, 8 * elem_count)
    places = deform_place[corner_node.reshape(-1)]
    node_count = stiff_diag.shape[2]
    every_value = lax.all_gather(values, ("dom", "sub"), axis=1, tiled=True)
    every_place = lax.all_gather(places, ("dom", "sub"), axis=0, tiled=True)
    node_slot = every_place - device * node_count
    owned = (node_slot >= 0) & (node_slot < node_count)
    node_slot = jnp.where(owned, node_slot, node_count)
    node_sens = jax.ops.segment_sum(every_value.T, node_slot, node_count + 1)[:node_count].T
    upper_term = jnp.einsum("abq,aq->bq", stiff_upper, node_sens, precision=precise)
    stacked = jnp.concatenate([upper_term, node_sens], 0)
    padded = padded_2(stacked, ((("dom", "sub"), 1),), 1)
    shape_grad = (
        jnp.einsum("abq,aq->bq", stiff_diag, node_sens, precision=precise) + padded[0:3, :-2]
    )
    shape_grad = shape_grad + jnp.einsum(
        "abq,aq->bq", stiff_lower, padded[3:6, 2:], precision=precise
    )
    return (adjoint, shape_grad)


def solution(mesh):
    placed = (
        P(("dom", "sub"), None),
        P(("dom", "sub"), None),
        P(None, ("dom", "sub"), None, None),
        P(("dom", "sub"), None, None),
        P(("dom", "sub"), None, None),
        P(("dom", "sub"), None),
        P(("dom", "sub"), None),
        P(),
        P(None, None, ("dom", "sub")),
        P(None, None, ("dom", "sub")),
        P(None, None, ("dom", "sub")),
    )
    return jax.shard_map(
        on_device,
        mesh=mesh,
        in_specs=placed,
        out_specs=(P(("dom", "sub"), None), P(None, ("dom", "sub"))),
        check_vma=False,
    )
```

profile of v0, /device:TPU:27, one launch (start us, length us, event | category | flops | bytes accessed | tf_op | source)
XLA Modules:
  0.0 206.3 jit_solution(1495273788116148652)
XLA Ops:
  0.7 0.8 slice_bitcast_fusion.24
  1.5 0.7 not_and_fusion
  2.2 0.7 convert_bitcast_fusion.1
  3.0 8.5 %fusion.2 = f32[12,1,6,320]{3,1,2,0:T(1,128)S(1)} fusion(bf16[6,12,320,320]{3,2,1,0:T(8,128)(2,1)} %param.13, bf16[12,320,1,1]{1,0,2,3:T(8,128)(2,1)S(1)} %convert_bitcast_fusion.1), kind=kOutput, calls=%fused_computation.4 | convolution fusion | flops 14745600 | bytes 14845440 | tf_op jit(solution)/shard_map/keij,ei->kej/dot_general | solution.py:91
  11.6 0.3 fusion.20
  11.9 2.6 %collective-permute-start.1 = (f32[12,320]{1,0:T(8,128)S(1)}, f32[12,320]{1,0:T(8,128)S(1)}, u32[]{:S(2)}, u32[]{:S(2)}) collective-permute-start(f32[12,320]{1,0:T(8,128)S(1)} %fusion.20), channel_id=1, source_target_pairs={{4,0},{8,4},{12,8},{16,12},{20,16},{24,20},{28,24},{5,1},{9,5},{13... | collective-permute-start | bytes 46088 | tf_op jit(solution)/shard_map/ppermute | solution.py:17
  14.9 1.3 collective-permute-start.2
  16.7 4.0 %collective-permute-start.3 = (f32[6,320]{1,0:T(8,128)S(1)}, f32[6,320]{1,0:T(8,128)S(1)}, u32[]{:S(2)}, u32[]{:S(2)}) collective-permute-start(f32[6,320]{1,0:T(8,128)S(1)} %fusion.18), channel_id=1, source_target_pairs={{1,0},{2,1},{3,2},{5,4},{6,5},{7,6},{9,8},{10,9},{11,10},{13,12},{... | collective-permute-start | bytes 23048 | tf_op jit(solution)/shard_map/ppermute | solution.py:17
  20.9 0.3 fusion.21
  21.1 4.4 %collective-permute-start = (f32[12,320]{1,0:T(8,128)S(1)}, f32[12,320]{1,0:T(8,128)S(1)}, u32[]{:S(2)}, u32[]{:S(2)}) collective-permute-start(f32[12,320]{1,0:T(8,128)S(1)} %fusion.21), channel_id=1, source_target_pairs={{0,4},{4,8},{8,12},{12,16},{16,20},{20,24},{24,28},{1,5},{5,9},{9,... | collective-permute-start | bytes 46088 | tf_op jit(solution)/shard_map/ppermute | solution.py:17
  26.6 1.0 gather_fusion
  27.6 0.3 dynamic-update-slice
  27.9 36.6 %all-reduce = s32[3072]{0:T(1024)S(1)} all-reduce(s32[3072]{0:T(1024)S(1)} %dynamic-update-slice), channel_id=2, replica_groups=mesh['dom'=8,'sub'=4] {'dom','sub'}, use_global_device_ids=true, to_apply=%add | all-reduce | flops 3072 | bytes 24576
  65.6 7.5 %fusion.29 = bf16[12,1,320]{2,1,0:T(2,128)(2,1)S(1)} fusion(f32[12,320,320]{2,1,0:T(8,128)} %param.14, f32[12,320,1]{1,0,2:T(8,128)S(1)} %fusion.13), kind=kOutput, calls=%fused_computation.48 | convolution fusion | flops 14745600 | bytes 4938240 | tf_op jit(solution)/shard_map/eij,ej->ei/dot_general | solution.py:103
  73.2 8.6 %fusion = f32[12,1,6,320]{3,1,2,0:T(1,128)S(1)} fusion(bf16[6,12,320,320]{3,2,1,0:T(8,128)(2,1)} %param.13, bf16[12,320,1,1]{1,0,2,3:T(8,128)(2,1)S(1)} %bitcast.130), kind=kOutput, calls=%fused_computation.2 | convolution fusion | flops 14745600 | bytes 14845440 | tf_op jit(solution)/shard_map/keij,ei->kej/dot_general | solution.py:91
  82.0 0.3 fusion.15
  82.3 0.3 fusion.17
  82.5 0.3 fusion.14
  82.8 1.3 collective-permute-start.6
  84.3 4.4 %collective-permute-start.5 = (f32[12,320]{1,0:T(8,128)S(1)}, f32[12,320]{1,0:T(8,128)S(1)}, u32[]{:S(2)}, u32[]{:S(2)}) collective-permute-start(f32[12,320]{1,0:T(8,128)S(1)} %fusion.16), channel_id=1, source_target_pairs={{4,0},{8,4},{12,8},{16,12},{20,16},{24,20},{28,24},{5,1},{9,5},{13... | collective-permute-start | bytes 46088 | tf_op jit(solution)/shard_map/ppermute | solution.py:17
  88.7 3.0 %collective-permute-start.4 = (f32[12,320]{1,0:T(8,128)S(1)}, f32[12,320]{1,0:T(8,128)S(1)}, u32[]{:S(2)}, u32[]{:S(2)}) collective-permute-start(f32[12,320]{1,0:T(8,128)S(1)} %fusion.17), channel_id=1, source_target_pairs={{0,4},{4,8},{8,12},{12,16},{16,20},{20,24},{24,28},{1,5},{5,9},{9,... | collective-permute-start | bytes 46088 | tf_op jit(solution)/shard_map/ppermute | solution.py:17
  91.8 4.4 %collective-permute-start.7 = (f32[6,320]{1,0:T(8,128)S(1)}, f32[6,320]{1,0:T(8,128)S(1)}, u32[]{:S(2)}, u32[]{:S(2)}) collective-permute-start(f32[6,320]{1,0:T(8,128)S(1)} %fusion.14), channel_id=1, source_target_pairs={{1,0},{2,1},{3,2},{5,4},{6,5},{7,6},{9,8},{10,9},{11,10},{13,12},{... | collective-permute-start | bytes 23048 | tf_op jit(solution)/shard_map/ppermute | solution.py:17
  96.4 0.4 collective-permute-done.7
  97.5 5.2 %fusion.26 = f32[12,1,320]{2,1,0:T(1,128)S(1)} fusion(f32[12,320,320]{2,1,0:T(8,128)S(1)} %bitcast.128, f32[12,320,1]{1,0,2:T(8,128)S(1)} %fusion.8), kind=kOutput, calls=%fused_computation.45 | convolution fusion | flops 14745600 | bytes 4945920 | tf_op jit(solution)/shard_map/eij,ej->ei/dot_general | solution.py:103
  102.7 0.6 convert_bitcast_fusion
  103.8 63.5 %all-gather.1 = f32[32,96,3]{1,2,0:T(4,128)S(1)} all-gather(f32[1,96,3]{1,2,0:T(4,128)S(1)} %bitcast.143), channel_id=1, replica_groups=mesh['dom'=8,'sub'=4] {'dom','sub'}, dimensions={0}, use_global_device_ids=true | all-gather | bytes 38016 | tf_op jit(solution)/shard_map/all_gather | solution.py:111
  167.4 0.5 copy.66
  167.9 21.1 %scatter_custom_fusion = f32[19,3]{1,0:T(8,128)S(1)} fusion(s32[3072]{0:T(1024)S(1)} %and_select_fusion, f32[3072,3]{1,0:T(8,128)S(1)} %bitcast.129, f32[]{:T(128)} %constant.34.clone.1), kind=kCustom, calls=%fused_computation.84 | custom fusion | flops 9216 | bytes 232 | tf_op jit(solution)/shard_map/scatter-add | solution.py:116
  189.3 7.8 %collective-permute-start.8 = (f32[6,1]{1,0:T(8,128)S(1)}, f32[6,1]{1,0:T(8,128)S(1)}, u32[]{:S(2)}, u32[]{:S(2)}) collective-permute-start(f32[6,1]{1,0:T(8,128)S(1)} %get-tuple-element.18), channel_id=1, source_target_pairs={{0,1},{1,2},{2,3},{3,4},{4,5},{5,6},{6,7},{7,8},{8,9},{9,10},{10,1... | collective-permute-start | bytes 80 | tf_op jit(solution)/shard_map/ppermute | solution.py:25
  197.1 1.9 collective-permute-start.9
  199.0 6.6 %collective-permute-done.9 = f32[6,1]{1,0:T(8,128)S(1)} collective-permute-done((f32[6,1]{1,0:T(8,128)S(1)}, f32[6,1]{1,0:T(8,128)S(1)}, u32[]{:S(2)}, u32[]{:S(2)}) %collective-permute-start.9) | collective-permute-done | bytes 56 | tf_op jit(solution)/shard_map/ppermute | solution.py:28
  205.8 0.6 bitcast_add_fusion
  (79 shorter events, 5.6 us)
Async XLA Ops:
  0.6 102.7 %copy-start = (bf16[12,24,320]{2,1,0:T(8,128)(2,1)S(1)}, bf16[12,24,320]{2,1,0:T(8,128)(2,1)}, u32[]{:S(2)}) copy-start(bf16[12,24,320]{2,1,0:T(8,128)(2,1)} %param.15) | copy-start | bytes 552964
  2.9 22.6 %copy-start.3 = (s32[12,6]{0,1:T(8,128)S(1)}, s32[12,6]{0,1:T(8,128)}, u32[]{:S(2)}) copy-start(s32[12,6]{0,1:T(8,128)} %param.16) | copy-start | bytes 868
  2.9 23.4 %copy-start.7 = (s32[12,8]{0,1:T(8,128)S(1)}, s32[12,8]{0,1:T(8,128)}, u32[]{:S(2)}) copy-start(s32[12,8]{0,1:T(8,128)} %param.17) | copy-start | bytes 1156
  2.9 23.6 %copy-start.1 = (s32[567]{0:T(1024)S(1)}, s32[567]{0:T(1024)}, u32[]{:S(2)}) copy-start(s32[567]{0:T(1024)} %param.18) | copy-start | bytes 6808
  3.0 62.4 %copy-start.2 = (f32[12,320]{1,0:T(8,128)S(1)}, f32[12,320]{1,0:T(8,128)}, u32[]{:S(2)}) copy-start(f32[12,320]{1,0:T(8,128)} %param.11) | copy-start | bytes 46084
  11.9 53.2 %collective-permute-start.1 = (f32[12,320]{1,0:T(8,128)S(1)}, f32[12,320]{1,0:T(8,128)S(1)}, u32[]{:S(2)}, u32[]{:S(2)}) collective-permute-start(f32[12,320]{1,0:T(8,128)S(1)} %fusion.20), channel_id=1, source_target_pairs={{4,0},{8,4},{12,8},{16,12},{20,16},{24,20},{28,24},{5,1},{9,5},{13... | collective-permute-start | bytes 46088 | tf_op jit(solution)/shard_map/ppermute | solution.py:17
  14.9 49.7 %collective-permute-start.2 = (f32[6,320]{1,0:T(8,128)S(1)}, f32[6,320]{1,0:T(8,128)S(1)}, u32[]{:S(2)}, u32[]{:S(2)}) collective-permute-start(f32[6,320]{1,0:T(8,128)S(1)} %fusion.19), channel_id=1, source_target_pairs={{0,1},{1,2},{2,3},{4,5},{5,6},{6,7},{8,9},{9,10},{10,11},{12,13},{... | collective-permute-start | bytes 23048 | tf_op jit(solution)/shard_map/ppermute | solution.py:17
  16.7 48.2 %collective-permute-start.3 = (f32[6,320]{1,0:T(8,128)S(1)}, f32[6,320]{1,0:T(8,128)S(1)}, u32[]{:S(2)}, u32[]{:S(2)}) collective-permute-start(f32[6,320]{1,0:T(8,128)S(1)} %fusion.18), channel_id=1, source_target_pairs={{1,0},{2,1},{3,2},{5,4},{6,5},{7,6},{9,8},{10,9},{11,10},{13,12},{... | collective-permute-start | bytes 23048 | tf_op jit(solution)/shard_map/ppermute | solution.py:17
  21.1 44.2 %collective-permute-start = (f32[12,320]{1,0:T(8,128)S(1)}, f32[12,320]{1,0:T(8,128)S(1)}, u32[]{:S(2)}, u32[]{:S(2)}) collective-permute-start(f32[12,320]{1,0:T(8,128)S(1)} %fusion.21), channel_id=1, source_target_pairs={{0,4},{4,8},{8,12},{12,16},{16,20},{20,24},{24,28},{1,5},{5,9},{9,... | collective-permute-start | bytes 46088 | tf_op jit(solution)/shard_map/ppermute | solution.py:17
  65.6 31.9 %slice-start = ((s8[5898240]{0:T(1024)(128)(4,1)}), s8[4194304]{0:T(1024)(128)(4,1)S(1)}, s32[]{:S(2)}) async-start(s8[5898240]{0:T(1024)(128)(4,1)} %bitcast.127), calls=%async_computation | async-start | bytes 8388608
  73.1 24.4 %slice-start.1 = ((s8[5898240]{0:T(1024)(128)(4,1)}), s8[1703936]{0:T(1024)(128)(4,1)S(1)}, s32[]{:S(2)}) async-start(s8[5898240]{0:T(1024)(128)(4,1)} %bitcast.127), calls=%async_computation.1 | async-start | bytes 3407872
  81.7 107.5 %copy-start.5 = (f32[3,3,18]{2,1,0:T(4,128)S(1)}, f32[3,3,18]{2,1,0:T(4,128)}, u32[]{:S(2)}) copy-start(f32[3,3,18]{2,1,0:T(4,128)} %param.19) | copy-start | bytes 1948
  81.7 107.5 %copy-start.6 = (f32[3,3,18]{2,1,0:T(4,128)S(1)}, f32[3,3,18]{2,1,0:T(4,128)}, u32[]{:S(2)}) copy-start(f32[3,3,18]{2,1,0:T(4,128)} %param.20) | copy-start | bytes 1948
  81.7 124.0 %copy-start.4 = (f32[3,3,18]{2,1,0:T(4,128)S(1)}, f32[3,3,18]{2,1,0:T(4,128)}, u32[]{:S(2)}) copy-start(f32[3,3,18]{2,1,0:T(4,128)} %param.21) | copy-start | bytes 1948
  82.8 13.4 %collective-permute-start.6 = (f32[6,320]{1,0:T(8,128)S(1)}, f32[6,320]{1,0:T(8,128)S(1)}, u32[]{:S(2)}, u32[]{:S(2)}) collective-permute-start(f32[6,320]{1,0:T(8,128)S(1)} %fusion.15), channel_id=1, source_target_pairs={{0,1},{1,2},{2,3},{4,5},{5,6},{6,7},{8,9},{9,10},{10,11},{12,13},{... | collective-permute-start | bytes 23048 | tf_op jit(solution)/shard_map/ppermute | solution.py:17
  84.3 12.7 %collective-permute-start.5 = (f32[12,320]{1,0:T(8,128)S(1)}, f32[12,320]{1,0:T(8,128)S(1)}, u32[]{:S(2)}, u32[]{:S(2)}) collective-permute-start(f32[12,320]{1,0:T(8,128)S(1)} %fusion.16), channel_id=1, source_target_pairs={{4,0},{8,4},{12,8},{16,12},{20,16},{24,20},{28,24},{5,1},{9,5},{13... | collective-permute-start | bytes 46088 | tf_op jit(solution)/shard_map/ppermute | solution.py:17
  88.7 8.5 %collective-permute-start.4 = (f32[12,320]{1,0:T(8,128)S(1)}, f32[12,320]{1,0:T(8,128)S(1)}, u32[]{:S(2)}, u32[]{:S(2)}) collective-permute-start(f32[12,320]{1,0:T(8,128)S(1)} %fusion.17), channel_id=1, source_target_pairs={{0,4},{4,8},{8,12},{12,16},{16,20},{20,24},{24,28},{1,5},{5,9},{9,... | collective-permute-start | bytes 46088 | tf_op jit(solution)/shard_map/ppermute | solution.py:17
  91.8 5.1 %collective-permute-start.7 = (f32[6,320]{1,0:T(8,128)S(1)}, f32[6,320]{1,0:T(8,128)S(1)}, u32[]{:S(2)}, u32[]{:S(2)}) collective-permute-start(f32[6,320]{1,0:T(8,128)S(1)} %fusion.14), channel_id=1, source_target_pairs={{1,0},{2,1},{3,2},{5,4},{6,5},{7,6},{9,8},{10,9},{11,10},{13,12},{... | collective-permute-start | bytes 23048 | tf_op jit(solution)/shard_map/ppermute | solution.py:17
  189.3 9.7 %collective-permute-start.8 = (f32[6,1]{1,0:T(8,128)S(1)}, f32[6,1]{1,0:T(8,128)S(1)}, u32[]{:S(2)}, u32[]{:S(2)}) collective-permute-start(f32[6,1]{1,0:T(8,128)S(1)} %get-tuple-element.18), channel_id=1, source_target_pairs={{0,1},{1,2},{2,3},{3,4},{4,5},{5,6},{6,7},{7,8},{8,9},{9,10},{10,1... | collective-permute-start | bytes 80 | tf_op jit(solution)/shard_map/ppermute | solution.py:25
  197.1 8.5 %collective-permute-start.9 = (f32[6,1]{1,0:T(8,128)S(1)}, f32[6,1]{1,0:T(8,128)S(1)}, u32[]{:S(2)}, u32[]{:S(2)}) collective-permute-start(f32[6,1]{1,0:T(8,128)S(1)} %get-tuple-element.19), channel_id=1, source_target_pairs={{1,0},{2,1},{3,2},{4,3},{5,4},{6,5},{7,6},{8,7},{9,8},{10,9},{11,1... | collective-permute-start | bytes 80 | tf_op jit(solution)/shard_map/ppermute | solution.py:28
where the time goes:
time: 207 us; the launch traced here: 206 us
  blocking collectives  100 us (48%)
  starting transfers between devices  35.1 us (17%)
  matrix products  34.2 us (17%)
  other arithmetic  25.4 us (12%)
  waiting for transfers between devices  7.03 us (3%)
  local copies, waits for them, and re-layouts  3.49 us (2%)
    all_gather x1, blocking collectives, on_device(): every_value = lax.all_gather(values, ('dom', 'sub'), axis=1, tiled=True)  63.5 us
    unnamed x1, blocking collectives  36.6 us
    ppermute x8, starting transfers between devices, passed_along(): lax.ppermute(value, axis, [(source, source + steps) for source in range(i...  25.4 us
    scatter-add x1, other arithmetic, on_device(): jax.ops.segment_sum(every_value.T, node_slot, node_count + 1)[:node_count]  21.1 us
    dot_general x2, matrix products, on_device(): jnp.einsum('keij,ei->kej', offdiag_blocks, rounded, preferred_element_typ...  17 us
    dot_general x2, matrix products, on_device(): jnp.einsum('eij,ej->ei', diag_inverse, adjoint_rhs - carried, precision=p...  12.8 us
    ppermute x1, starting transfers between devices, padded_2(): lax.ppermute(lax.slice_in_dim(block, block.shape[dim] - width, None, axis...  7.75 us
    ppermute x1, waiting for transfers between devices, padded_2(): lax.ppermute(lax.slice_in_dim(block, 0, width, axis=dim), axis, backward)  6.58 us
  transfers between devices with their start and end apart: 10, of which 2 were waited for; matrix products, arithmetic and copies ran while one was open for 3% of the time, Pallas kernels for 0%

commit v1 on v0

--- a/solution.py
+++ b/solution.py
@@ -9,6 +9,28 @@
 BZ = 6
 SWEEPS = 2
 precise = lax.Precision.HIGHEST
+
+
+def treat_page_all(mat, dim_no):
+    r1 = list(mat.shape[1:])
+    r1[dim_no] *= mat.shape[0]
+    return jnp.moveaxis(mat, 0, dim_no).reshape(r1)
+
+
+def wait_quarters_on(shard_in, across):
+    carry_in = shard_in[None]
+    n_axis = lax.axis_size(across)
+    for dd in range(n_axis.bit_length() - 1):
+        b_next = 1 << dd
+        later = lax.ppermute(
+            carry_in,
+            axis_name=across,
+            perm=list(map(lambda tick: (tick, tick ^ b_next), range(n_axis))),
+        )
+        reached = jnp.stack([carry_in, later])
+        top = lax.axis_index(across) >> dd & 1
+        carry_in = jnp.where(top == 0, reached, reached[::-1]).reshape(-1, *shard_in.shape)
+    return carry_in
 
 
 def passed_along(value, axis, steps):
@@ -65,6 +87,10 @@
     stiff_upper,
     stiff_lower,
 ):
+
+    def shape_links_all(x_in, message, at_axis):
+        return treat_page_all(wait_quarters_on(x_in, message), at_axis)
+
     elem_count = adjoint_rhs.shape[0]
     block_size = adjoint_rhs.shape[1]
     device = lax.axis_index(("dom", "sub"))
@@ -108,7 +134,7 @@
     values = corner_terms.reshape(elem_count, 8, 3).transpose(2, 0, 1).reshape(3, 8 * elem_count)
     places = deform_place[corner_node.reshape(-1)]
     node_count = stiff_diag.shape[2]
-    every_value = lax.all_gather(values, ("dom", "sub"), axis=1, tiled=True)
+    every_value = shape_links_all(values, ("dom", "sub"), 1)
     every_place = lax.all_gather(places, ("dom", "sub"), axis=0, tiled=True)
     node_slot = every_place - device * node_count
     owned = (node_slot >= 0) & (node_slot < node_count)

time: 207 us -> 158 us (0.76)
  blocking collectives: 100 us -> 41.3 us
  starting transfers between devices: 35.1 us -> 40 us
  waiting for transfers between devices: 7.03 us -> 11.8 us
    all_gather x1 -> x0, blocking collectives: 63.5 us -> none  [on_device(): every_value = lax.all_gather(values, ('dom', 'sub'), axis=1, tiled=True)]
    ppermute x0 -> x5, starting transfers between devices: none -> 5.92 us  [wait_quarters_on(): lax.ppermute(carry_in, axis_name=across, perm=list(map(lambda tick: (tick...]
    ppermute x0 -> x5, waiting for transfers between devices: none -> 4.77 us  [wait_quarters_on(): lax.ppermute(carry_in, axis_name=across, perm=list(map(lambda tick: (tick...]
    unnamed x1, blocking collectives: 36.6 us -> 41.3 us
  transfers between devices with their start and end apart: 10 -> 15, of which waited for: 2 -> 6; matrix products, arithmetic and copies ran while one was open for 3% -> 3% of each run, Pallas kernels for 0% -> 0%
where the time goes in v1:
time: 158 us; the launch traced here: 157 us
  blocking collectives  41.3 us (26%)
  starting transfers between devices  40 us (25%)
  matrix products  34.1 us (22%)
  other arithmetic  25.5 us (16%)
  waiting for transfers between devices  11.8 us (7%)
  local copies, waits for them, and re-layouts  3.61 us (2%)
    unnamed x1, blocking collectives  41.3 us
    ppermute x8, starting transfers between devices, passed_along(): lax.ppermute(value, axis, [(source, source + steps) for source in range(i...  24.3 us
    scatter-add x1, other arithmetic, on_device(): jax.ops.segment_sum(every_value.T, node_slot, node_count + 1)[:node_count]  21.1 us
    dot_general x2, matrix products, on_device(): jnp.einsum('keij,ei->kej', offdiag_blocks, rounded, preferred_element_typ...  17 us
    dot_general x2, matrix products, on_device(): jnp.einsum('eij,ej->ei', diag_inverse, adjoint_rhs - carried, precision=p...  12.8 us
    ppermute x1, starting transfers between devices, padded_2(): lax.ppermute(lax.slice_in_dim(block, block.shape[dim] - width, None, axis...  7.79 us
    ppermute x1, waiting for transfers between devices, padded_2(): lax.ppermute(lax.slice_in_dim(block, 0, width, axis=dim), axis, backward)  6.58 us
    ppermute x5, starting transfers between devices, wait_quarters_on(): lax.ppermute(carry_in, axis_name=across, perm=list(map(lambda tick: (tick...  5.92 us
  transfers between devices with their start and end apart: 15, of which 6 were waited for; matrix products, arithmetic and copies ran while one was open for 3% of the time, Pallas kernels for 0%

profile of v1, /device:TPU:27, one launch (start us, length us, event | category | flops | bytes accessed | tf_op | source)
XLA Modules:
  0.0 157.3 jit_solution(4877667678205106190)
XLA Ops:
  0.7 0.8 slice_bitcast_fusion.24
  1.5 0.7 not_and_fusion
  2.2 0.7 convert_bitcast_fusion.1
  2.9 8.4 %fusion.2 = f32[12,1,6,320]{3,1,2,0:T(1,128)S(1)} fusion(bf16[6,12,320,320]{3,2,1,0:T(8,128)(2,1)} %param.13, bf16[12,320,1,1]{1,0,2,3:T(8,128)(2,1)S(1)} %convert_bitcast_fusion.1), kind=kOutput, calls=%fused_computation.4 | convolution fusion | flops 14745600 | bytes 14845440 | tf_op jit(solution)/shard_map/keij,ei->kej/dot_general | solution.py:117
  11.9 2.6 %collective-permute-start.1 = (f32[12,320]{1,0:T(8,128)S(1)}, f32[12,320]{1,0:T(8,128)S(1)}, u32[]{:S(2)}, u32[]{:S(2)}) collective-permute-start(f32[12,320]{1,0:T(8,128)S(1)} %fusion.20), channel_id=1, source_target_pairs={{4,0},{8,4},{12,8},{16,12},{20,16},{24,20},{28,24},{5,1},{9,5},{13... | collective-permute-start | bytes 46088 | tf_op jit(solution)/shard_map/ppermute | solution.py:39
  14.9 1.3 collective-permute-start.2
  16.7 4.0 %collective-permute-start.3 = (f32[6,320]{1,0:T(8,128)S(1)}, f32[6,320]{1,0:T(8,128)S(1)}, u32[]{:S(2)}, u32[]{:S(2)}) collective-permute-start(f32[6,320]{1,0:T(8,128)S(1)} %fusion.18), channel_id=1, source_target_pairs={{1,0},{2,1},{3,2},{5,4},{6,5},{7,6},{9,8},{10,9},{11,10},{13,12},{... | collective-permute-start | bytes 23048 | tf_op jit(solution)/shard_map/ppermute | solution.py:39
  21.1 4.4 %collective-permute-start = (f32[12,320]{1,0:T(8,128)S(1)}, f32[12,320]{1,0:T(8,128)S(1)}, u32[]{:S(2)}, u32[]{:S(2)}) collective-permute-start(f32[12,320]{1,0:T(8,128)S(1)} %fusion.21), channel_id=1, source_target_pairs={{0,4},{4,8},{8,12},{12,16},{16,20},{20,24},{24,28},{1,5},{5,9},{9,... | collective-permute-start | bytes 46088 | tf_op jit(solution)/shard_map/ppermute | solution.py:39
  27.4 7.5 %fusion.31 = bf16[12,1,320]{2,1,0:T(2,128)(2,1)S(1)} fusion(f32[12,320,320]{2,1,0:T(8,128)} %param.14, f32[12,320,1]{1,0,2:T(8,128)S(1)} %fusion.13), kind=kOutput, calls=%fused_computation.55 | convolution fusion | flops 14745600 | bytes 4938240 | tf_op jit(solution)/shard_map/eij,ej->ei/dot_general | solution.py:129
  35.0 8.6 %fusion = f32[12,1,6,320]{3,1,2,0:T(1,128)S(1)} fusion(bf16[6,12,320,320]{3,2,1,0:T(8,128)(2,1)} %param.13, bf16[12,320,1,1]{1,0,2,3:T(8,128)(2,1)S(1)} %bitcast.150), kind=kOutput, calls=%fused_computation.2 | convolution fusion | flops 14745600 | bytes 14845440 | tf_op jit(solution)/shard_map/keij,ei->kej/dot_general | solution.py:117
  44.7 1.3 collective-permute-start.6
  46.2 1.9 %collective-permute-start.5 = (f32[12,320]{1,0:T(8,128)S(1)}, f32[12,320]{1,0:T(8,128)S(1)}, u32[]{:S(2)}, u32[]{:S(2)}) collective-permute-start(f32[12,320]{1,0:T(8,128)S(1)} %fusion.16), channel_id=1, source_target_pairs={{4,0},{8,4},{12,8},{16,12},{20,16},{24,20},{28,24},{5,1},{9,5},{13... | collective-permute-start | bytes 46088 | tf_op jit(solution)/shard_map/ppermute | solution.py:39
  48.2 4.5 %collective-permute-start.4 = (f32[12,320]{1,0:T(8,128)S(1)}, f32[12,320]{1,0:T(8,128)S(1)}, u32[]{:S(2)}, u32[]{:S(2)}) collective-permute-start(f32[12,320]{1,0:T(8,128)S(1)} %fusion.17), channel_id=1, source_target_pairs={{0,4},{4,8},{8,12},{12,16},{16,20},{20,24},{24,28},{1,5},{5,9},{9,... | collective-permute-start | bytes 46088 | tf_op jit(solution)/shard_map/ppermute | solution.py:39
  52.7 4.3 %collective-permute-start.7 = (f32[6,320]{1,0:T(8,128)S(1)}, f32[6,320]{1,0:T(8,128)S(1)}, u32[]{:S(2)}, u32[]{:S(2)}) collective-permute-start(f32[6,320]{1,0:T(8,128)S(1)} %fusion.14), channel_id=1, source_target_pairs={{1,0},{2,1},{3,2},{5,4},{6,5},{7,6},{9,8},{10,9},{11,10},{13,12},{... | collective-permute-start | bytes 23048 | tf_op jit(solution)/shard_map/ppermute | solution.py:39
  58.3 5.2 %fusion.28 = f32[12,1,320]{2,1,0:T(1,128)S(1)} fusion(f32[12,320,320]{2,1,0:T(8,128)S(1)} %bitcast.147, f32[12,320,1]{1,0,2:T(8,128)S(1)} %fusion.8), kind=kOutput, calls=%fused_computation.52 | convolution fusion | flops 14745600 | bytes 4945920 | tf_op jit(solution)/shard_map/eij,ej->ei/dot_general | solution.py:129
  63.5 0.6 convert_bitcast_fusion
  64.6 1.8 %collective-permute-start.8 = (f32[1,3,96]{2,1,0:T(4,128)S(1)}, f32[1,3,96]{2,1,0:T(4,128)S(1)}, u32[]{:S(2)}, u32[]{:S(2)}) collective-permute-start(f32[1,3,96]{2,1,0:T(4,128)S(1)} %broadcast_in_dim_reshape.3), channel_id=1, source_target_pairs={{0,1},{1,0},{2,3},{3,2},{4,5},{5,4},{6,7},{7,6},{8,9},{9,8},{10,11... | collective-permute-start | bytes 3464 | tf_op jit(solution)/shard_map/ppermute | solution.py:25
  66.5 0.9 collective-permute-done.8
  67.4 1.4 collective-permute-start.9
  69.0 1.8 %collective-permute-done.9 = f32[2,3,96]{2,1,0:T(4,128)S(1)} collective-permute-done((f32[2,3,96]{2,1,0:T(4,128)S(1)}, f32[2,3,96]{2,1,0:T(4,128)S(1)}, u32[]{:S(2)}, u32[]{:S(2)}) %collective-permute-start.9) | collective-permute-done | bytes 2336 | tf_op jit(solution)/shard_map/ppermute | solution.py:25
  70.8 1.0 collective-permute-start.10
  71.9 0.8 collective-permute-done.10
  72.8 1.0 gather_fusion
  74.1 41.3 %all-reduce = s32[3072]{0:T(1024)S(1)} all-reduce(s32[3072]{0:T(1024)S(1)} %dynamic-update-slice), channel_id=2, replica_groups=mesh['dom'=8,'sub'=4] {'dom','sub'}, use_global_device_ids=true, to_apply=%add | all-reduce | flops 3072 | bytes 24576
  115.4 1.6 %collective-permute-start.12 = (f32[16,3,96]{2,0,1:T(8,128)S(1)}, f32[16,3,96]{2,0,1:T(8,128)S(1)}, u32[]{:S(2)}, u32[]{:S(2)}) collective-permute-start(f32[16,3,96]{2,0,1:T(8,128)S(1)} %get-tuple-element.13), channel_id=1, source_target_pairs={{0,16},{1,17},{2,18},{3,19},{4,20},{5,21},{6,22},{7,23},{8,24},{9,... | collective-permute-start | bytes 55304 | tf_op jit(solution)/shard_map/ppermute | solution.py:25
  117.1 1.2 collective-permute-done.12
  118.3 0.5 copy.78
  118.8 21.1 %scatter_custom_fusion = f32[19,3]{1,0:T(8,128)S(1)} fusion(s32[3072]{0:T(1024)S(1)} %and_select_fusion, f32[3072,3]{1,0:T(8,128)S(1)} %bitcast.148, f32[]{:T(128)} %constant.37.clone.1), kind=kCustom, calls=%fused_computation.95 | custom fusion | flops 9216 | bytes 232 | tf_op jit(solution)/shard_map/scatter-add | solution.py:142
  140.3 7.8 %collective-permute-start.13 = (f32[6,1]{1,0:T(8,128)S(1)}, f32[6,1]{1,0:T(8,128)S(1)}, u32[]{:S(2)}, u32[]{:S(2)}) collective-permute-start(f32[6,1]{1,0:T(8,128)S(1)} %get-tuple-element.18), channel_id=1, source_target_pairs={{0,1},{1,2},{2,3},{3,4},{4,5},{5,6},{6,7},{7,8},{8,9},{9,10},{10,1... | collective-permute-start | bytes 80 | tf_op jit(solution)/shard_map/ppermute | solution.py:47
  148.1 1.9 %collective-permute-start.14 = (f32[6,1]{1,0:T(8,128)S(1)}, f32[6,1]{1,0:T(8,128)S(1)}, u32[]{:S(2)}, u32[]{:S(2)}) collective-permute-start(f32[6,1]{1,0:T(8,128)S(1)} %get-tuple-element.19), channel_id=1, source_target_pairs={{1,0},{2,1},{3,2},{4,3},{5,4},{6,5},{7,6},{8,7},{9,8},{10,9},{11,1... | collective-permute-start | bytes 80 | tf_op jit(solution)/shard_map/ppermute | solution.py:50
  150.0 6.6 %collective-permute-done.14 = f32[6,1]{1,0:T(8,128)S(1)} collective-permute-done((f32[6,1]{1,0:T(8,128)S(1)}, f32[6,1]{1,0:T(8,128)S(1)}, u32[]{:S(2)}, u32[]{:S(2)}) %collective-permute-start.14) | collective-permute-done | bytes 56 | tf_op jit(solution)/shard_map/ppermute | solution.py:50
  156.8 0.6 bitcast_add_fusion
  (102 shorter events, 7.9 us)
Async XLA Ops:
  0.6 63.5 %copy-start = (bf16[12,24,320]{2,1,0:T(8,128)(2,1)S(1)}, bf16[12,24,320]{2,1,0:T(8,128)(2,1)}, u32[]{:S(2)}) copy-start(bf16[12,24,320]{2,1,0:T(8,128)(2,1)} %param.15) | copy-start | bytes 552964
  2.9 22.6 %copy-start.3 = (s32[12,6]{0,1:T(8,128)S(1)}, s32[12,6]{0,1:T(8,128)}, u32[]{:S(2)}) copy-start(s32[12,6]{0,1:T(8,128)} %param.16) | copy-start | bytes 868
  2.9 24.3 %copy-start.2 = (f32[12,320]{1,0:T(8,128)S(1)}, f32[12,320]{1,0:T(8,128)}, u32[]{:S(2)}) copy-start(f32[12,320]{1,0:T(8,128)} %param.11) | copy-start | bytes 46084
  11.9 15.1 %collective-permute-start.1 = (f32[12,320]{1,0:T(8,128)S(1)}, f32[12,320]{1,0:T(8,128)S(1)}, u32[]{:S(2)}, u32[]{:S(2)}) collective-permute-start(f32[12,320]{1,0:T(8,128)S(1)} %fusion.20), channel_id=1, source_target_pairs={{4,0},{8,4},{12,8},{16,12},{20,16},{24,20},{28,24},{5,1},{9,5},{13... | collective-permute-start | bytes 46088 | tf_op jit(solution)/shard_map/ppermute | solution.py:39
  14.9 11.7 %collective-permute-start.2 = (f32[6,320]{1,0:T(8,128)S(1)}, f32[6,320]{1,0:T(8,128)S(1)}, u32[]{:S(2)}, u32[]{:S(2)}) collective-permute-start(f32[6,320]{1,0:T(8,128)S(1)} %fusion.19), channel_id=1, source_target_pairs={{0,1},{1,2},{2,3},{4,5},{5,6},{6,7},{8,9},{9,10},{10,11},{12,13},{... | collective-permute-start | bytes 23048 | tf_op jit(solution)/shard_map/ppermute | solution.py:39
  16.7 10.1 %collective-permute-start.3 = (f32[6,320]{1,0:T(8,128)S(1)}, f32[6,320]{1,0:T(8,128)S(1)}, u32[]{:S(2)}, u32[]{:S(2)}) collective-permute-start(f32[6,320]{1,0:T(8,128)S(1)} %fusion.18), channel_id=1, source_target_pairs={{1,0},{2,1},{3,2},{5,4},{6,5},{7,6},{9,8},{10,9},{11,10},{13,12},{... | collective-permute-start | bytes 23048 | tf_op jit(solution)/shard_map/ppermute | solution.py:39
  21.1 6.1 %collective-permute-start = (f32[12,320]{1,0:T(8,128)S(1)}, f32[12,320]{1,0:T(8,128)S(1)}, u32[]{:S(2)}, u32[]{:S(2)}) collective-permute-start(f32[12,320]{1,0:T(8,128)S(1)} %fusion.21), channel_id=1, source_target_pairs={{0,4},{4,8},{8,12},{12,16},{16,20},{20,24},{24,28},{1,5},{5,9},{9,... | collective-permute-start | bytes 46088 | tf_op jit(solution)/shard_map/ppermute | solution.py:39
  27.4 30.8 %slice-start = ((s8[5898240]{0:T(1024)(128)(4,1)}), s8[4194304]{0:T(1024)(128)(4,1)S(1)}, s32[]{:S(2)}) async-start(s8[5898240]{0:T(1024)(128)(4,1)} %bitcast.146), calls=%async_computation | async-start | bytes 8388608
  35.0 23.3 %slice-start.1 = ((s8[5898240]{0:T(1024)(128)(4,1)}), s8[1703936]{0:T(1024)(128)(4,1)S(1)}, s32[]{:S(2)}) async-start(s8[5898240]{0:T(1024)(128)(4,1)} %bitcast.146), calls=%async_computation.1 | async-start | bytes 3407872
  43.6 25.2 %copy-start.7 = (s32[12,8]{0,1:T(8,128)S(1)}, s32[12,8]{0,1:T(8,128)}, u32[]{:S(2)}) copy-start(s32[12,8]{0,1:T(8,128)} %param.17) | copy-start | bytes 1156
  43.6 29.2 %copy-start.1 = (s32[567]{0:T(1024)S(1)}, s32[567]{0:T(1024)}, u32[]{:S(2)}) copy-start(s32[567]{0:T(1024)} %param.18) | copy-start | bytes 6808
  43.6 96.6 %copy-start.5 = (f32[3,3,18]{2,1,0:T(4,128)S(1)}, f32[3,3,18]{2,1,0:T(4,128)}, u32[]{:S(2)}) copy-start(f32[3,3,18]{2,1,0:T(4,128)} %param.19) | copy-start | bytes 1948
  43.6 96.6 %copy-start.6 = (f32[3,3,18]{2,1,0:T(4,128)S(1)}, f32[3,3,18]{2,1,0:T(4,128)}, u32[]{:S(2)}) copy-start(f32[3,3,18]{2,1,0:T(4,128)} %param.20) | copy-start | bytes 1948
  43.6 113.1 %copy-start.4 = (f32[3,3,18]{2,1,0:T(4,128)S(1)}, f32[3,3,18]{2,1,0:T(4,128)}, u32[]{:S(2)}) copy-start(f32[3,3,18]{2,1,0:T(4,128)} %param.21) | copy-start | bytes 1948
  44.7 12.3 %collective-permute-start.6 = (f32[6,320]{1,0:T(8,128)S(1)}, f32[6,320]{1,0:T(8,128)S(1)}, u32[]{:S(2)}, u32[]{:S(2)}) collective-permute-start(f32[6,320]{1,0:T(8,128)S(1)} %fusion.15), channel_id=1, source_target_pairs={{0,1},{1,2},{2,3},{4,5},{5,6},{6,7},{8,9},{9,10},{10,11},{12,13},{... | collective-permute-start | bytes 23048 | tf_op jit(solution)/shard_map/ppermute | solution.py:39
  46.2 11.6 %collective-permute-start.5 = (f32[12,320]{1,0:T(8,128)S(1)}, f32[12,320]{1,0:T(8,128)S(1)}, u32[]{:S(2)}, u32[]{:S(2)}) collective-permute-start(f32[12,320]{1,0:T(8,128)S(1)} %fusion.16), channel_id=1, source_target_pairs={{4,0},{8,4},{12,8},{16,12},{20,16},{24,20},{28,24},{5,1},{9,5},{13... | collective-permute-start | bytes 46088 | tf_op jit(solution)/shard_map/ppermute | solution.py:39
  48.2 9.9 %collective-permute-start.4 = (f32[12,320]{1,0:T(8,128)S(1)}, f32[12,320]{1,0:T(8,128)S(1)}, u32[]{:S(2)}, u32[]{:S(2)}) collective-permute-start(f32[12,320]{1,0:T(8,128)S(1)} %fusion.17), channel_id=1, source_target_pairs={{0,4},{4,8},{8,12},{12,16},{16,20},{20,24},{24,28},{1,5},{5,9},{9,... | collective-permute-start | bytes 46088 | tf_op jit(solution)/shard_map/ppermute | solution.py:39
  52.7 4.9 %collective-permute-start.7 = (f32[6,320]{1,0:T(8,128)S(1)}, f32[6,320]{1,0:T(8,128)S(1)}, u32[]{:S(2)}, u32[]{:S(2)}) collective-permute-start(f32[6,320]{1,0:T(8,128)S(1)} %fusion.14), channel_id=1, source_target_pairs={{1,0},{2,1},{3,2},{5,4},{6,5},{7,6},{9,8},{10,9},{11,10},{13,12},{... | collective-permute-start | bytes 23048 | tf_op jit(solution)/shard_map/ppermute | solution.py:39
  64.6 2.8 %collective-permute-start.8 = (f32[1,3,96]{2,1,0:T(4,128)S(1)}, f32[1,3,96]{2,1,0:T(4,128)S(1)}, u32[]{:S(2)}, u32[]{:S(2)}) collective-permute-start(f32[1,3,96]{2,1,0:T(4,128)S(1)} %broadcast_in_dim_reshape.3), channel_id=1, source_target_pairs={{0,1},{1,0},{2,3},{3,2},{4,5},{5,4},{6,7},{7,6},{8,9},{9,8},{10,11... | collective-permute-start | bytes 3464 | tf_op jit(solution)/shard_map/ppermute | solution.py:25
  67.4 3.4 %collective-permute-start.9 = (f32[2,3,96]{2,1,0:T(4,128)S(1)}, f32[2,3,96]{2,1,0:T(4,128)S(1)}, u32[]{:S(2)}, u32[]{:S(2)}) collective-permute-start(f32[2,3,96]{2,1,0:T(4,128)S(1)} %get-tuple-element.21), channel_id=1, source_target_pairs={{0,2},{1,3},{2,0},{3,1},{4,6},{5,7},{6,4},{7,5},{8,10},{9,11},{10,... | collective-permute-start | bytes 6920 | tf_op jit(solution)/shard_map/ppermute | solution.py:25
  70.8 1.8 %collective-permute-start.10 = (f32[4,3,96]{2,1,0:T(4,128)S(1)}, f32[4,3,96]{2,1,0:T(4,128)S(1)}, u32[]{:S(2)}, u32[]{:S(2)}) collective-permute-start(f32[4,3,96]{2,1,0:T(4,128)S(1)} %bitcast.163), channel_id=1, source_target_pairs={{0,4},{1,5},{2,6},{3,7},{4,0},{5,1},{6,2},{7,3},{8,12},{9,13},{10,... | collective-permute-start | bytes 13832 | tf_op jit(solution)/shard_map/ppermute | solution.py:25
  72.7 42.7 %collective-permute-start.11 = (f32[8,3,96]{2,0,1:T(8,128)S(1)}, f32[8,3,96]{2,0,1:T(8,128)S(1)}, u32[]{:S(2)}, u32[]{:S(2)}) collective-permute-start(f32[8,3,96]{2,0,1:T(8,128)S(1)} %copy.41), channel_id=1, source_target_pairs={{0,8},{1,9},{2,10},{3,11},{4,12},{5,13},{6,14},{7,15},{8,0},{9,1},... | collective-permute-start | bytes 27656 | tf_op jit(solution)/shard_map/ppermute | solution.py:25
  115.4 2.9 %collective-permute-start.12 = (f32[16,3,96]{2,0,1:T(8,128)S(1)}, f32[16,3,96]{2,0,1:T(8,128)S(1)}, u32[]{:S(2)}, u32[]{:S(2)}) collective-permute-start(f32[16,3,96]{2,0,1:T(8,128)S(1)} %get-tuple-element.13), channel_id=1, source_target_pairs={{0,16},{1,17},{2,18},{3,19},{4,20},{5,21},{6,22},{7,23},{8,24},{9,... | collective-permute-start | bytes 55304 | tf_op jit(solution)/shard_map/ppermute | solution.py:25
  140.3 9.7 %collective-permute-start.13 = (f32[6,1]{1,0:T(8,128)S(1)}, f32[6,1]{1,0:T(8,128)S(1)}, u32[]{:S(2)}, u32[]{:S(2)}) collective-permute-start(f32[6,1]{1,0:T(8,128)S(1)} %get-tuple-element.18), channel_id=1, source_target_pairs={{0,1},{1,2},{2,3},{3,4},{4,5},{5,6},{6,7},{7,8},{8,9},{9,10},{10,1... | collective-permute-start | bytes 80 | tf_op jit(solution)/shard_map/ppermute | solution.py:47
  148.1 8.5 %collective-permute-start.14 = (f32[6,1]{1,0:T(8,128)S(1)}, f32[6,1]{1,0:T(8,128)S(1)}, u32[]{:S(2)}, u32[]{:S(2)}) collective-permute-start(f32[6,1]{1,0:T(8,128)S(1)} %get-tuple-element.19), channel_id=1, source_target_pairs={{1,0},{2,1},{3,2},{4,3},{5,4},{6,5},{7,6},{8,7},{9,8},{10,9},{11,1... | collective-permute-start | bytes 80 | tf_op jit(solution)/shard_map/ppermute | solution.py:50
